TPU v7x, 32 devices: a whole 2x2x4 slice. The times are simulated.
32 devices in a mesh: loop: 8 (over z, x), rep: 4 (over y, core).
Axes of the slice: x: 2, y: 2, z: 4, core: 2. Of those that a mesh axis runs over, the one named last changes fastest.
Arguments:
- features: float32 [4096, 128], P('loop'), may hold values from -6 to 6
- weight: float32 [128, 256], replicated, may hold values from -0.5 to 0.5
- bias: float32 [256], replicated, may hold values from -3 to 3
- tile_values: float32 [512, 128, 128], P(('loop', 'rep')), may hold values from -0.125 to 0.125
- tile_rows: int32 [512], P(('loop', 'rep')), may hold values from 0 to 31, as said below
- tile_cols: int32 [512], P(('loop', 'rep')), may hold values from 0 to 31, as said below
- tile_count: int32 [32], P(('loop', 'rep')), may hold values from 1 to 16, as said below
- cotangent: float32 [4096, 256], P('loop'), may hold values from -0.6 to 0.6
Outputs:
- output: float32 [4096, 256], P('loop')
- grad_features: float32 [4096, 128], P('loop')
- grad_weight: float32 [128, 256], replicated
- grad_bias: float32 [256], replicated
Inputs may be any that keep to these rules, and one draw needn't show every extreme that they name: `tile_rows`: every slot of a device at loop index l names a row block from l * 4 to (l + 1) * 4 - 1. `tile_cols`: for every loop index m, the live slots of one device name at most 2 different column blocks from m * 4 to (m + 1) * 4 - 1; for every loop index some device names exactly 2 of one such range. `tile_count`: for every loop index some device has all 16 slots live.
All inputs are finite; a program needn't handle non-finite values.
Results may differ from a plain program's by a relative error of at most 0.0001.
Values sent between devices are 32-bit elements; how exact they have to be, the bound alone decides.
No kernel may reach another device: no remote copies, remote signals or barrier semaphores. Data moves between devices by JAX's collectives and lax.ppermute only.
A program may use at most 64 MiB of HBM per device.

v0:
```python
import jax
import jax.numpy as jnp
from jax import lax
from jax.sharding import PartitionSpec as P


def per_device(features, weight, bias, tile_values, tile_rows, tile_cols, tile_count, cotangent):
    highest = lax.Precision.HIGHEST
    tile_side = tile_values.shape[1]
    rows_here = features.shape[0]
    nblocks = rows_here // tile_side
    slots = tile_values.shape[0]
    local_rows = tile_rows - lax.axis_index("loop") * nblocks
    live_slot = (jnp.arange(slots, dtype=jnp.int32) < tile_count[0]).astype(jnp.float32)
    row_pick = (local_rows[:, None] == jnp.arange(nblocks, dtype=jnp.int32)[None, :]).astype(
        jnp.float32
    )
    row_pick = row_pick * live_slot[:, None]
    gathered = lax.all_gather(features, "loop", axis=0, tiled=True)
    width = gathered.shape[1]
    blocks = gathered.reshape(-1, tile_side, width)[tile_cols]
    products = jnp.einsum("kij,kjf->kif", tile_values, blocks, precision=highest)
    aggregated = lax.psum(
        jnp.einsum("kb,kif->bif", row_pick, products, precision=highest), "rep"
    ).reshape(rows_here, -1)
    preactive = jnp.dot(aggregated, weight, precision=highest) + bias
    logistic = jax.nn.sigmoid(preactive)
    output = preactive * logistic
    gradient = cotangent * logistic * (1.0 + preactive * (1.0 - logistic))
    spread = jnp.dot(gradient, weight.T, precision=highest)
    source_blocks = spread.reshape(nblocks, tile_side, spread.shape[1])[
        jnp.clip(local_rows, 0, nblocks - 1)
    ]
    outgoing = jnp.einsum("kji,kjf->kif", tile_values, source_blocks, precision=highest)
    outgoing = outgoing * live_slot[:, None, None]
    span = rows_here * lax.axis_size("loop") // tile_side + 2
    column_pick = (tile_cols[:, None] == jnp.arange(span, dtype=jnp.int32)[None, :]).astype(
        jnp.float32
    )
    placed = jnp.einsum("kb,kif->bif", column_pick, outgoing, precision=highest)
    placed = placed.reshape(span * tile_side, outgoing.shape[2])
    term = lax.psum_scatter(
        lax.slice_in_dim(placed, 0, rows_here * lax.axis_size("loop"), axis=0),
        "loop",
        scatter_dimension=0,
        tiled=True,
    )
    own_rows = lax.psum(term, "rep")
    weight_term = jnp.dot(aggregated.T, gradient, precision=highest)
    bias_term = jnp.sum(gradient, axis=0)
    grad_weight, grad_bias = lax.psum((weight_term, bias_term), "loop")
    return (output, own_rows, grad_weight, grad_bias)


def solution(mesh):
    return jax.shard_map(
        per_device,
        mesh=mesh,
        in_specs=(
            P("loop", None),
            P(),
            P(),
            P(("loop", "rep"), None, None),
            P(("loop", "rep")),
            P(("loop", "rep")),
            P(("loop", "rep")),
            P("loop", None),
        ),
        out_specs=(P("loop", None), P("loop", None), P(), P()),
        check_vma=False,
    )
```

profile of v0, /device:TPU:0, one launch (start us, length us, event | category | flops | bytes accessed | tf_op | source)
XLA Modules:
  0.0 293.9 jit_solution(1856292996977088046)
XLA Ops:
  7.2 0.0 copy-start
  7.2 0.0 all-gather.2.cloned.1.call-start
  7.2 0.7 all-gather.2.cloned.1.call-update
  7.9 0.0 all-reduce.4.cloned.1.call-start
  8.6 0.7 compare_select_fusion.1
  9.3 0.7 compare_select_fusion
  10.0 52.0 %all-gather.2.cloned.1.call-done = f32[4096,128]{1,0:T(8,128)} async-done(((f32[512,128]{1,0:T(8,128)}), f32[4096,128]{1,0:T(8,128)}) %all-gather.2.cloned.1.call-update) | async-done | bytes 2097168 | tf_op jit(solution)/shard_map/all_gather | solution.py:19
  62.0 2.2 gather_fusion
  64.2 0.0 copy-done
  64.2 1.8 fusion.16
  66.0 0.0 copy-start.5
  66.0 0.0 copy-start.4
  66.0 0.0 copy-start.7
  66.1 0.5 copy.14
  66.6 0.0 copy-start.6
  66.6 0.6 fusion.2
  67.2 0.7 copy.12
  67.9 0.0 all-reduce.4.cloned.1.call-update
  68.0 0.0 reduce-scatter.2.cloned.1.call-start
  68.0 0.0 copy-done.5
  68.0 0.1 fusion.7
  68.1 30.8 %all-reduce.4.cloned.1.call-done = f32[512,128]{1,0:T(8,128)} async-done(((f32[512,128]{1,0:T(8,128)}), f32[512,128]{1,0:T(8,128)}) %all-reduce.4.cloned.1.call-update) | async-done | bytes 262160 | tf_op jit(solution)/shard_map/psum | solution.py:23
  98.9 0.0 copy-done.4
  98.9 0.0 copy-done.7
  98.9 0.0 copy-done.6
  98.9 2.5 fusion.15
  101.4 0.0 copy-start.1
  101.4 0.6 fusion.17
  102.0 0.2 copy-done.1
  102.2 0.6 gather_fusion.1
  102.8 1.8 fusion.18
  104.7 0.5 copy.15
  105.2 1.0 fusion
  106.2 2.6 copy.13
  108.8 0.0 reduce-scatter.2.cloned.1.call-update
  108.8 0.0 all-reduce.8.cloned.1.call-start
  108.9 1.0 copy-done.2
  109.8 0.1 copy-done.3
  109.9 1.3 fusion.19
  111.2 0.0 all-reduce.8.cloned.1.call-update
  111.2 0.0 all-reduce.6.cloned.1.call-start
  111.3 66.0 %reduce-scatter.2.cloned.1.call-done = f32[512,128]{1,0:T(8,128)} async-done(((f32[4096,128]{1,0:T(8,128)}), f32[512,128]{1,0:T(8,128)}) %reduce-scatter.2.cloned.1.call-update) | async-done | bytes 262160 | tf_op jit(solution)/shard_map/reduce_scatter | solution.py:42
  177.3 0.0 all-reduce.6.cloned.1.call-update
  177.3 19.7 %psum.31 = f32[256]{0:T(256)} all-reduce(f32[256]{0:T(256)S(1)} %get-tuple-element.4), channel_id=1, replica_groups=mesh['loop'=8,'rep'=4] {'loop'}, use_global_device_ids=true, to_apply=%region_5.6 | all-reduce | flops 256 | bytes 2048 | tf_op jit(solution)/shard_map/psum | solution.py:51
  197.0 53.6 %all-reduce.8.cloned.1.call-done = f32[128,256]{1,0:T(8,128)} async-done(((f32[128,256]{1,0:T(8,128)}), f32[128,256]{1,0:T(8,128)}) %all-reduce.8.cloned.1.call-update) | async-done | bytes 131088 | tf_op jit(solution)/shard_map/psum | solution.py:51
  250.6 33.6 %all-reduce.6.cloned.1.call-done = f32[512,128]{1,0:T(8,128)} async-done(((f32[512,128]{1,0:T(8,128)}), f32[512,128]{1,0:T(8,128)}) %all-reduce.6.cloned.1.call-update) | async-done | bytes 262160 | tf_op jit(solution)/shard_map/psum | solution.py:48
  284.2 1.7 copy.20
  285.8 1.6 copy.21
  (5 shorter events, 0.0 us)
Async XLA Ops:
  7.2 57.0 %copy-start = (f32[16,128,128]{2,1,0:T(8,128)S(1)}, f32[16,128,128]{2,1,0:T(8,128)}, u32[]{:S(2)}) copy-start(f32[16,128,128]{2,1,0:T(8,128)} %param.11) | copy-start | bytes 3145732
  7.2 54.8 %all-gather.2.cloned.1.call-start = ((), (), s32[]{:S(2)}) async-start(), calls=%async_computation.1 | async-start | bytes 2359296 | tf_op jit(solution)/shard_map/all_gather | solution.py:19
  7.9 91.0 %all-reduce.4.cloned.1.call-start = ((), (), s32[]{:S(2)}) async-start(), calls=%async_computation.2 | async-start | bytes 524288 | tf_op jit(solution)/shard_map/psum | solution.py:23
  66.0 2.0 copy-start.5
  66.0 32.9 %copy-start.4 = (f32[128,256]{1,0:T(8,128)S(1)}, f32[128,256]{1,0:T(8,128)}, u32[]{:S(2)}) copy-start(f32[128,256]{1,0:T(8,128)} %param.9) | copy-start | bytes 393220
  66.0 32.9 %copy-start.7 = (f32[256]{0:T(256)S(1)}, f32[256]{0:T(256)}, u32[]{:S(2)}) copy-start(f32[256]{0:T(256)} %param.10) | copy-start | bytes 3076
  66.6 32.4 %copy-start.6 = (f32[512,256]{1,0:T(8,128)S(1)}, f32[512,256]{1,0:T(8,128)}, u32[]{:S(2)}) copy-start(f32[512,256]{1,0:T(8,128)} %param.15) | copy-start | bytes 1572868
  68.0 109.3 %reduce-scatter.2.cloned.1.call-start = ((), (), s32[]{:S(2)}) async-start(), calls=%async_computation.3 | async-start | bytes 2359296 | tf_op jit(solution)/shard_map/reduce_scatter | solution.py:42
  101.4 0.8 copy-start.1
  108.8 1.0 copy-start.2
  108.8 1.1 copy-start.3
  108.8 141.7 %all-reduce.8.cloned.1.call-start = ((), (), s32[]{:S(2)}) async-start(), calls=%async_computation.5 | async-start | bytes 262144 | tf_op jit(solution)/shard_map/psum | solution.py:51
  111.2 173.0 %all-reduce.6.cloned.1.call-start = ((), (), s32[]{:S(2)}) async-start(), calls=%async_computation.4 | async-start | bytes 524288 | tf_op jit(solution)/shard_map/psum | solution.py:48
Sparse Core Ops, SparseCore 0:
  10.1 51.7 all-gather.1
  68.1 30.8 all-reduce.3
  108.9 68.2 reduce-scatter.1
  181.0 69.4 all-reduce.7
  252.7 31.3 all-reduce.5
where the time goes:
time: 294 us
  waiting for transfers between devices  237 us (81%)
  blocking collectives  19.7 us (7%)
  between operations  14.6 us (5%)
  local copies, waits for them, and re-layouts  11.6 us (4%)
  matrix products  9.66 us (3%)
    reduce_scatter x1, waiting for transfers between devices, per_device(): lax.psum_scatter(lax.slice_in_dim(placed, 0, rows_here * lax.axis_size('l...  66 us
    psum x1, waiting for transfers between devices, per_device(): grad_weight, grad_bias = lax.psum((weight_term, bias_term), 'loop')  53.6 us
    all_gather x1, waiting for transfers between devices, per_device(): gathered = lax.all_gather(features, 'loop', axis=0, tiled=True)  52 us
    psum x1, waiting for transfers between devices, per_device(): own_rows = lax.psum(term, 'rep')  33.6 us
    psum x1, waiting for transfers between devices, per_device(): lax.psum(jnp.einsum('kb,kif->bif', row_pick, products, precision=highest)...  30.8 us
    psum x1, blocking collectives, per_device(): grad_weight, grad_bias = lax.psum((weight_term, bias_term), 'loop')  19.7 us
  transfers between devices with their start and end apart: 5, of which 5 were waited for; matrix products, arithmetic and copies ran while one was open for 1% of the time, Pallas kernels for 0%

commit v1 on v0

--- a/solution.py
+++ b/solution.py
@@ -16,7 +16,12 @@
         jnp.float32
     )
     row_pick = row_pick * live_slot[:, None]
-    gathered = lax.all_gather(features, "loop", axis=0, tiled=True)
+    ring = [features]
+    for hop in range(7):
+        ring.append(lax.ppermute(ring[-1], "loop", [(dev, (dev + 1) % 8) for dev in range(8)]))
+    gathered = jnp.roll(
+        jnp.concatenate(ring[::-1], axis=0), (lax.axis_index("loop") + 1) * ring[0].shape[0], axis=0
+    )
     width = gathered.shape[1]
     blocks = gathered.reshape(-1, tile_side, width)[tile_cols]
     products = jnp.einsum("kij,kjf->kif", tile_values, blocks, precision=highest)

time: 294 us -> 310 us (1.054)
  waiting for transfers between devices: 237 us -> 248 us
    ppermute x0 -> x7, waiting for transfers between devices: none -> 63.9 us  [per_device(): lax.ppermute(ring[-1], 'loop', [(dev, (dev + 1) % 8) for dev in range(8)])]
    all_gather x1 -> x0, waiting for transfers between devices: 52 us -> none  [per_device(): gathered = lax.all_gather(features, 'loop', axis=0, tiled=True)]
  transfers between devices with their start and end apart: 5 -> 11, of which waited for: 5 -> 11; matrix products, arithmetic and copies ran while one was open for 1% -> 1% of each run, Pallas kernels for 0% -> 0%
where the time goes in v1:
time: 310 us; the launch traced here: 309 us
  waiting for transfers between devices  248 us (80%)
  blocking collectives  19.8 us (6%)
  between operations  14.7 us (5%)
  local copies, waits for them, and re-layouts  11.4 us (4%)
  matrix products  11.1 us (4%)
  starting transfers between devices  3.2 us (1%)
    reduce_scatter x1, waiting for transfers between devices, per_device(): lax.psum_scatter(lax.slice_in_dim(placed, 0, rows_here * lax.axis_size('l...  66.9 us
    ppermute x7, waiting for transfers between devices, per_device(): lax.ppermute(ring[-1], 'loop', [(dev, (dev + 1) % 8) for dev in range(8)])  63.9 us
    psum x1, waiting for transfers between devices, per_device(): grad_weight, grad_bias = lax.psum((weight_term, bias_term), 'loop')  53.8 us
    psum x1, waiting for transfers between devices, per_device(): own_rows = lax.psum(term, 'rep')  33.6 us
    psum x1, waiting for transfers between devices, per_device(): lax.psum(jnp.einsum('kb,kif->bif', row_pick, products, precision=highest)...  29.4 us
    psum x1, blocking collectives, per_device(): grad_weight, grad_bias = lax.psum((weight_term, bias_term), 'loop')  19.8 us
  transfers between devices with their start and end apart: 11, of which 11 were waited for; matrix products, arithmetic and copies ran while one was open for 1% of the time, Pallas kernels for 0%

profile of v1, /device:TPU:0, one launch (start us, length us, event | category | flops | bytes accessed | tf_op | source)
XLA Modules:
  0.0 309.2 jit_solution(10311011979975898362)
XLA Ops:
  7.2 0.0 copy-start
  7.2 0.0 copy-start.3
  7.2 0.0 all-reduce.4.cloned.1.call-start
  7.2 3.0 collective-permute-start
  10.3 9.6 %collective-permute-done = f32[512,128]{1,0:T(8,128)S(1)} collective-permute-done((f32[512,128]{1,0:T(8,128)}, f32[512,128]{1,0:T(8,128)S(1)}, u32[]{:S(2)}, u32[]{:S(2)}) %collective-permute-start) | collective-permute-done | bytes 262176 | tf_op jit(solution)/shard_map/ppermute | solution.py:21
  19.8 0.0 collective-permute-start.1
  19.8 10.2 %collective-permute-done.1 = f32[512,128]{1,0:T(8,128)S(1)} collective-permute-done((f32[512,128]{1,0:T(8,128)S(1)}, f32[512,128]{1,0:T(8,128)S(1)}, u32[]{:S(2)}, u32[]{:S(2)}) %collective-permute-start.1) | collective-permute-done | bytes 262176 | tf_op jit(solution)/shard_map/ppermute | solution.py:21
  30.0 0.0 collective-permute-start.2
  30.0 9.3 %collective-permute-done.2 = f32[512,128]{1,0:T(8,128)S(1)} collective-permute-done((f32[512,128]{1,0:T(8,128)S(1)}, f32[512,128]{1,0:T(8,128)S(1)}, u32[]{:S(2)}, u32[]{:S(2)}) %collective-permute-start.2) | collective-permute-done | bytes 262176 | tf_op jit(solution)/shard_map/ppermute | solution.py:21
  39.3 0.0 collective-permute-start.3
  39.3 9.1 %collective-permute-done.3 = f32[512,128]{1,0:T(8,128)S(1)} collective-permute-done((f32[512,128]{1,0:T(8,128)S(1)}, f32[512,128]{1,0:T(8,128)S(1)}, u32[]{:S(2)}, u32[]{:S(2)}) %collective-permute-start.3) | collective-permute-done | bytes 262176 | tf_op jit(solution)/shard_map/ppermute | solution.py:21
  48.4 0.0 collective-permute-start.4
  48.4 9.1 %collective-permute-done.4 = f32[512,128]{1,0:T(8,128)S(1)} collective-permute-done((f32[512,128]{1,0:T(8,128)S(1)}, f32[512,128]{1,0:T(8,128)S(1)}, u32[]{:S(2)}, u32[]{:S(2)}) %collective-permute-start.4) | collective-permute-done | bytes 262176 | tf_op jit(solution)/shard_map/ppermute | solution.py:21
  57.4 0.7 compare_select_fusion
  58.1 9.0 %collective-permute-done.5 = f32[512,128]{1,0:T(8,128)S(1)} collective-permute-done((f32[512,128]{1,0:T(8,128)S(1)}, f32[512,128]{1,0:T(8,128)S(1)}, u32[]{:S(2)}, u32[]{:S(2)}) %collective-permute-start.5) | collective-permute-done | bytes 262176 | tf_op jit(solution)/shard_map/ppermute | solution.py:21
  67.1 0.7 compare_select_fusion.1
  68.5 7.7 %collective-permute-done.6 = f32[512,128]{1,0:T(8,128)S(1)} collective-permute-done((f32[512,128]{1,0:T(8,128)S(1)}, f32[512,128]{1,0:T(8,128)S(1)}, u32[]{:S(2)}, u32[]{:S(2)}) %collective-permute-start.6) | collective-permute-done | bytes 262176 | tf_op jit(solution)/shard_map/ppermute | solution.py:21
  76.4 1.0 constant_dynamic-update-slice_fusion.8
  77.6 0.1 constant_dynamic-slice_fusion
  77.7 1.6 gather_fusion
  79.3 3.1 %fusion.16 = f32[16,128,128]{2,1,0:T(8,128)S(1)} fusion(f32[16,128,128]{2,1,0:T(8,128)} %gather_fusion, f32[16,128,128]{2,1,0:T(8,128)S(1)} %copy-done), kind=kOutput, calls=%fused_computation.46 | convolution fusion | flops 402653184 | bytes 3145728 | tf_op jit(solution)/shard_map/kij,kjf->kif/dot_general | solution.py:27
  82.4 0.5 copy.14
  82.9 0.6 fusion.2
  83.6 0.7 copy.12
  84.3 0.0 all-reduce.4.cloned.1.call-update
  84.3 0.0 reduce-scatter.2.cloned.1.call-start
  84.4 0.1 fusion.7
  84.5 29.4 %all-reduce.4.cloned.1.call-done = f32[512,128]{1,0:T(8,128)} async-done(((f32[512,128]{1,0:T(8,128)}), f32[512,128]{1,0:T(8,128)}) %all-reduce.4.cloned.1.call-update) | async-done | bytes 262160 | tf_op jit(solution)/shard_map/psum | solution.py:28
  113.9 2.6 fusion.15
  116.5 0.6 fusion.17
  117.1 0.2 copy-done.1
  117.3 0.6 gather_fusion.1
  117.9 1.8 fusion.18
  119.8 0.5 copy.15
  120.3 1.0 fusion
  121.4 2.5 copy.13
  123.9 0.0 reduce-scatter.2.cloned.1.call-update
  123.9 0.0 all-reduce.8.cloned.1.call-start
  124.0 1.3 fusion.19
  125.3 0.0 all-reduce.8.cloned.1.call-update
  125.3 0.0 all-reduce.6.cloned.1.call-start
  125.3 66.9 %reduce-scatter.2.cloned.1.call-done = f32[512,128]{1,0:T(8,128)} async-done(((f32[4096,128]{1,0:T(8,128)}), f32[512,128]{1,0:T(8,128)}) %reduce-scatter.2.cloned.1.call-update) | async-done | bytes 262160 | tf_op jit(solution)/shard_map/reduce_scatter | solution.py:47
  192.3 0.0 all-reduce.6.cloned.1.call-update
  192.3 19.8 %psum.31 = f32[256]{0:T(256)} all-reduce(f32[256]{0:T(256)S(1)} %get-tuple-element.4), channel_id=1, replica_groups=mesh['loop'=8,'rep'=4] {'loop'}, use_global_device_ids=true, to_apply=%region_5.6 | all-reduce | flops 256 | bytes 2048 | tf_op jit(solution)/shard_map/psum | solution.py:56
  212.1 53.8 %all-reduce.8.cloned.1.call-done = f32[128,256]{1,0:T(8,128)} async-done(((f32[128,256]{1,0:T(8,128)}), f32[128,256]{1,0:T(8,128)}) %all-reduce.8.cloned.1.call-update) | async-done | bytes 131088 | tf_op jit(solution)/shard_map/psum | solution.py:56
  265.9 33.6 %all-reduce.6.cloned.1.call-done = f32[512,128]{1,0:T(8,128)} async-done(((f32[512,128]{1,0:T(8,128)}), f32[512,128]{1,0:T(8,128)}) %all-reduce.6.cloned.1.call-update) | async-done | bytes 262160 | tf_op jit(solution)/shard_map/psum | solution.py:53
  299.5 1.7 copy.35
  301.1 1.6 copy.36
  (32 shorter events, 0.3 us)
Async XLA Ops:
  7.2 72.2 %copy-start = (f32[16,128,128]{2,1,0:T(8,128)S(1)}, f32[16,128,128]{2,1,0:T(8,128)}, u32[]{:S(2)}) copy-start(f32[16,128,128]{2,1,0:T(8,128)} %param.11) | copy-start | bytes 3145732
  7.2 70.4 %copy-start.3 = (f32[512,128]{1,0:T(8,128)S(1)}, f32[512,128]{1,0:T(8,128)}, u32[]{:S(2)}) copy-start(f32[512,128]{1,0:T(8,128)} %param.8) | copy-start | bytes 786436
  7.2 106.7 %all-reduce.4.cloned.1.call-start = ((), (), s32[]{:S(2)}) async-start(), calls=%async_computation.1 | async-start | bytes 524288 | tf_op jit(solution)/shard_map/psum | solution.py:28
  7.2 12.6 %collective-permute-start = (f32[512,128]{1,0:T(8,128)}, f32[512,128]{1,0:T(8,128)S(1)}, u32[]{:S(2)}, u32[]{:S(2)}) collective-permute-start(f32[512,128]{1,0:T(8,128)} %param.8), channel_id=1, source_target_pairs={{0,4},{4,8},{8,12},{12,16},{16,20},{20,24},{24,28},{28,0},{1,5},{5... | collective-permute-start | bytes 786440 | tf_op jit(solution)/shard_map/ppermute | solution.py:21
  19.8 10.2 %collective-permute-start.1 = (f32[512,128]{1,0:T(8,128)S(1)}, f32[512,128]{1,0:T(8,128)S(1)}, u32[]{:S(2)}, u32[]{:S(2)}) collective-permute-start(f32[512,128]{1,0:T(8,128)S(1)} %collective-permute-done), channel_id=1, source_target_pairs={{0,4},{4,8},{8,12},{12,16},{16,20},{20,24},{24,28},{28,0},{1,5},{5... | collective-permute-start | bytes 786440 | tf_op jit(solution)/shard_map/ppermute | solution.py:21
  30.0 9.3 %collective-permute-start.2 = (f32[512,128]{1,0:T(8,128)S(1)}, f32[512,128]{1,0:T(8,128)S(1)}, u32[]{:S(2)}, u32[]{:S(2)}) collective-permute-start(f32[512,128]{1,0:T(8,128)S(1)} %collective-permute-done.1), channel_id=1, source_target_pairs={{0,4},{4,8},{8,12},{12,16},{16,20},{20,24},{24,28},{28,0},{1,5},{5... | collective-permute-start | bytes 786440 | tf_op jit(solution)/shard_map/ppermute | solution.py:21
  39.3 9.1 %collective-permute-start.3 = (f32[512,128]{1,0:T(8,128)S(1)}, f32[512,128]{1,0:T(8,128)S(1)}, u32[]{:S(2)}, u32[]{:S(2)}) collective-permute-start(f32[512,128]{1,0:T(8,128)S(1)} %collective-permute-done.2), channel_id=1, source_target_pairs={{0,4},{4,8},{8,12},{12,16},{16,20},{20,24},{24,28},{28,0},{1,5},{5... | collective-permute-start | bytes 786440 | tf_op jit(solution)/shard_map/ppermute | solution.py:21
  48.4 9.1 %collective-permute-start.4 = (f32[512,128]{1,0:T(8,128)S(1)}, f32[512,128]{1,0:T(8,128)S(1)}, u32[]{:S(2)}, u32[]{:S(2)}) collective-permute-start(f32[512,128]{1,0:T(8,128)S(1)} %collective-permute-done.3), channel_id=1, source_target_pairs={{0,4},{4,8},{8,12},{12,16},{16,20},{20,24},{24,28},{28,0},{1,5},{5... | collective-permute-start | bytes 786440 | tf_op jit(solution)/shard_map/ppermute | solution.py:21
  57.4 9.7 %collective-permute-start.5 = (f32[512,128]{1,0:T(8,128)S(1)}, f32[512,128]{1,0:T(8,128)S(1)}, u32[]{:S(2)}, u32[]{:S(2)}) collective-permute-start(f32[512,128]{1,0:T(8,128)S(1)} %collective-permute-done.4), channel_id=1, source_target_pairs={{0,4},{4,8},{8,12},{12,16},{16,20},{20,24},{24,28},{28,0},{1,5},{5... | collective-permute-start | bytes 786440 | tf_op jit(solution)/shard_map/ppermute | solution.py:21
  67.1 9.1 %collective-permute-start.6 = (f32[512,128]{1,0:T(8,128)S(1)}, f32[512,128]{1,0:T(8,128)S(1)}, u32[]{:S(2)}, u32[]{:S(2)}) collective-permute-start(f32[512,128]{1,0:T(8,128)S(1)} %collective-permute-done.5), channel_id=1, source_target_pairs={{0,4},{4,8},{8,12},{12,16},{16,20},{20,24},{24,28},{28,0},{1,5},{5... | collective-permute-start | bytes 786440 | tf_op jit(solution)/shard_map/ppermute | solution.py:21
  79.3 5.1 %copy-start.6 = (s32[16]{0:T(128)S(1)}, s32[16]{0:T(128)}, u32[]{:S(2)}) copy-start(s32[16]{0:T(128)} %param.13) | copy-start | bytes 196
  79.3 34.5 %copy-start.5 = (f32[128,256]{1,0:T(8,128)S(1)}, f32[128,256]{1,0:T(8,128)}, u32[]{:S(2)}) copy-start(f32[128,256]{1,0:T(8,128)} %param.9) | copy-start | bytes 393220
  79.3 34.5 %copy-start.7 = (f32[256]{0:T(256)S(1)}, f32[256]{0:T(256)}, u32[]{:S(2)}) copy-start(f32[256]{0:T(256)} %param.10) | copy-start | bytes 3076
  84.3 108.0 %reduce-scatter.2.cloned.1.call-start = ((), (), s32[]{:S(2)}) async-start(), calls=%async_computation.2 | async-start | bytes 2359296 | tf_op jit(solution)/shard_map/reduce_scatter | solution.py:47
  116.5 0.8 copy-start.1
  120.3 3.7 %copy-start.2 = (f32[512,256]{1,0:T(8,128)S(1)}, f32[512,256]{1,0:T(8,128)}, u32[]{:S(2)}) copy-start(f32[512,256]{1,0:T(8,128)} %copy-done.1) | copy-start | bytes 1572868
  120.3 3.7 %copy-start.4 = (f32[512,128]{1,0:T(8,128)S(1)}, f32[512,128]{1,0:T(8,128)}, u32[]{:S(2)}) copy-start(f32[512,128]{1,0:T(8,128)} %all-reduce.4.cloned.1.call-done) | copy-start | bytes 786436
  123.9 141.9 %all-reduce.8.cloned.1.call-start = ((), (), s32[]{:S(2)}) async-start(), calls=%async_computation.4 | async-start | bytes 262144 | tf_op jit(solution)/shard_map/psum | solution.py:56
  125.3 174.2 %all-reduce.6.cloned.1.call-start = ((), (), s32[]{:S(2)}) async-start(), calls=%async_computation.3 | async-start | bytes 524288 | tf_op jit(solution)/shard_map/psum | solution.py:53
Sparse Core Ops, SparseCore 0:
  84.4 29.3 all-reduce.3
  124.1 68.1 reduce-scatter.1
  196.2 69.6 all-reduce.7
  268.0 31.3 all-reduce.5
